TPU v7x, 256 devices: a whole 4x4x8 slice. The times are simulated.
256 devices in a mesh: outer: 32 (over z, x), inner: 8 (over y, core).
Axes of the slice: x: 4, y: 4, z: 8, core: 2. Of those that a mesh axis runs over, the one named last changes fastest.
Arguments:
- query: bfloat16 [32768, 32, 128], P(('outer', 'inner')), may hold values from -6 to 6
- keys: bfloat16 [32768, 32, 128], P(('outer', 'inner')), may hold values from -6 to 6
- value: bfloat16 [32768, 32, 128], P(('outer', 'inner')), may hold values from -6 to 6
- beta: bfloat16 [32768, 32], P(('outer', 'inner')), may hold values from 0 to 1, as said below
Outputs:
- mixed: bfloat16 [32768, 32, 128], P(('outer', 'inner'))
Inputs may be any that keep to these rules, and one draw needn't show every extreme that they name: `beta`: each gate lies strictly between 0 and 1.
All inputs are finite; a program needn't handle non-finite values.
Results may differ from a plain program's by a relative error of at most 0.001.
Values may be sent and summed in bfloat16 or wider, within the bound.
No kernel may reach another device: no remote copies, remote signals or barrier semaphores. Data moves between devices by JAX's collectives and lax.ppermute only.
A program may use at most 128 MiB of HBM per device.

v0:
```python
import jax
import jax.numpy as jnp
from jax import lax
from jax.sharding import PartitionSpec as P

SPAN = 128
HIGH = lax.Precision.HIGHEST


def prefix(x, axis, combine, identity):
    peers, index = (lax.axis_size(axis), lax.axis_index(axis))
    everything = jax.tree.map(lambda part: lax.all_gather(part, axis), x)
    start = jax.tree.map(
        lambda part, zero: jnp.broadcast_to(jnp.asarray(zero, part.dtype), part.shape), x, identity
    )

    def step(k, before):
        reached = k < index
        new = combine(before, jax.tree.map(lambda part: part[k], everything))
        return jax.tree.map(lambda a, b: jnp.where(reached, a, b), new, before)

    return lax.fori_loop(0, peers, step, start)


def unit_rows(block):
    return block * lax.rsqrt(jnp.sum(block * block, axis=-1, keepdims=True) + 1e-06)


def unit_lower_inverse(strict_part):
    size = strict_part.shape[0]
    inverse = jnp.eye(size, dtype=jnp.float32) - strict_part
    power = jnp.dot(strict_part, strict_part, precision=HIGH)
    for level in range((size - 1).bit_length() - 1):
        inverse = inverse + jnp.dot(inverse, power, precision=HIGH)
        power = jnp.dot(power, power, precision=HIGH)
    return inverse


def span_terms(query_block, keys_c, value_c, beta_c):
    width = keys_c.shape[1]
    query_block = query_block.astype(jnp.float32)
    keys_c = keys_c.astype(jnp.float32)
    value_c = value_c.astype(jnp.float32)
    beta_c = beta_c.astype(jnp.float32)
    qnorm = unit_rows(query_block)
    knorm = unit_rows(keys_c)
    kbeta = knorm * beta_c[:, None]
    vbeta = value_c * beta_c[:, None]
    gram = jnp.dot(kbeta, knorm.T, precision=HIGH)
    inverse = unit_lower_inverse(jnp.tril(gram, -1))
    solved = jnp.dot(inverse, jnp.concatenate([kbeta, vbeta], axis=1), precision=HIGH)
    weights = solved[:, :width]
    updates = solved[:, width:]
    scores = jnp.tril(jnp.dot(qnorm, knorm.T, precision=HIGH))
    return (qnorm, knorm, weights, updates, scores)


def combine_pairs(earlier, later):
    trans_a, offset_a = earlier
    trans_b, offset_b = later
    merged = jnp.einsum("hij,hjk->hik", trans_b, trans_a, precision=HIGH)
    shifted = jnp.einsum("hij,hjk->hik", trans_b, offset_a, precision=HIGH) + offset_b
    return (merged, shifted)


def shards(query, keys, value, beta):
    qhead, khead, vhead, bhead = (
        lax.all_to_all(query, "inner", split_axis=1, concat_axis=0, tiled=True),
        lax.all_to_all(keys, "inner", split_axis=1, concat_axis=0, tiled=True),
        lax.all_to_all(value, "inner", split_axis=1, concat_axis=0, tiled=True),
        lax.all_to_all(beta, "inner", split_axis=1, concat_axis=0, tiled=True),
    )
    length, groups, width = qhead.shape
    count = length // SPAN

    def blocks(array):
        return jnp.transpose(array.reshape(count, SPAN, groups, width), (0, 2, 1, 3))

    bblk = jnp.transpose(bhead.reshape(count, SPAN, groups), (0, 2, 1))
    terms_fn = jax.vmap(jax.vmap(span_terms))
    qnorm, knorm, weights, updates, scores = terms_fn(
        blocks(qhead), blocks(khead), blocks(vhead), bblk
    )
    eye = jnp.broadcast_to(jnp.eye(width, dtype=jnp.float32), (groups, width, width))
    zeros = jnp.zeros((groups, width, width), jnp.float32)
    joined_parts = jnp.concatenate([eye, zeros], axis=2)

    def pair_step(carried, kpart, wpart, upart):
        product = jnp.einsum("hcd,hde->hce", wpart, carried, precision=HIGH)
        change = jnp.concatenate([-product[..., :width], upart - product[..., width:]], axis=2)
        nextpair = carried + jnp.einsum("hcd,hce->hde", kpart, change, precision=HIGH)
        return (nextpair, change)

    def transition_only(carried, inputs):
        kpart, wpart, upart = inputs
        nextpair, change = pair_step(carried, kpart, wpart, upart)
        return (nextpair, None)

    final_pair, _ = lax.scan(transition_only, joined_parts, (knorm, weights, updates))
    block_trans = final_pair[..., :width]
    block_offset = final_pair[..., width:]
    _, incoming = prefix((block_trans, block_offset), "outer", combine_pairs, (eye, zeros))

    def advance(state, inputs):
        qpart, kpart, wpart, upart, spart = inputs
        delta = upart - jnp.einsum("hcd,hde->hce", wpart, state, precision=HIGH)
        result = jnp.einsum("hcd,hde->hce", qpart, state, precision=HIGH) + jnp.einsum(
            "hcs,hse->hce", spart, delta, precision=HIGH
        )
        state = state + jnp.einsum("hcd,hce->hde", kpart, delta, precision=HIGH)
        return (state, result.astype(jnp.bfloat16))

    _, outputs = lax.scan(advance, incoming, (qnorm, knorm, weights, updates, scores))
    token_major = jnp.transpose(outputs, (0, 2, 1, 3)).reshape(length, groups, width)
    return lax.all_to_all(token_major, "inner", split_axis=0, concat_axis=1, tiled=True)


def solution(mesh):
    placed = (
        P(("outer", "inner"), None, None),
        P(("outer", "inner"), None, None),
        P(("outer", "inner"), None, None),
        P(("outer", "inner"), None),
    )
    return jax.shard_map(
        shards,
        mesh=mesh,
        in_specs=placed,
        out_specs=P(("outer", "inner"), None, None),
        check_vma=False,
    )
```

profile of v0, /device:TPU:1, one launch (start us, length us, event | category | flops | bytes accessed | tf_op | source)
XLA Modules:
  0.0 445.4 jit_solution(17959281910144616222)
XLA Ops:
  6.5 6.5 %all-to-all-start.1 = ((bf16[128,8,4]{0,2,1:T(4,128)(2,1)}), bf16[128,8,4]{0,2,1:T(4,128)(2,1)S(1)}, u32[]{:S(2)}, u32[]{:S(2)}) async-start(bf16[128,8,4]{0,2,1:T(4,128)(2,1)} %bitcast.145), calls=%async_computation.1 | async-start | bytes 16384 | tf_op jit(solution)/shard_map/all_to_all | solution.py:71
  13.0 2.7 copy.24
  17.6 4.2 all-to-all-start
  23.4 13.5 %all-to-all-done = bf16[128,32,128]{2,0,1:T(8,128)(2,1)S(1)} async-done(((bf16[128,32,128]{2,0,1:T(8,128)(2,1)}), bf16[128,32,128]{2,0,1:T(8,128)(2,1)S(1)}, u32[]{:S(2)}, u32[]{:S(2)}) %all-to-all-start) | async-done | bytes 1048608 | tf_op jit(solution)/shard_map/all_to_all | solution.py:69
  36.9 4.3 all-to-all-start.2
  41.9 6.5 %fusion.57 = f32[8,4,128,128]{3,2,1,0:T(8,128)S(1)} fusion(bf16[128,8,4,128]{3,0,2,1:T(8,128)(2,1)S(1)} %bitcast.135, f32[8,4,128]{2,1,0:T(4,128)S(1)} %add_rsqrt_fusion.1, f32[8,4,128]{2,1,0:T(4,128)S(1)} %convert_bitcast_fusion.3), kind=kOutput, calls=%fused_computation.68 | convolution fusion | flops 807927808 | bytes 3178496 | tf_op jit(solution)/shard_map/vmap(vmap())/dot_general | solution.py:49
  48.4 2.2 fusion.51
  50.6 2.5 subtract_add_fusion
  53.0 2.0 fusion.75
  55.1 2.0 fusion.77
  57.1 2.2 fusion.76
  59.3 2.2 fusion.78
  61.5 2.3 convolution_add_fusion.5
  63.8 2.0 fusion.80
  65.8 2.2 fusion.79
  68.0 2.0 fusion.81
  70.1 2.5 convolution_add_fusion.4
  73.9 3.5 fusion.82
  77.4 2.2 fusion.59
  80.4 4.3 fusion.35
  84.7 2.6 fusion.73
  87.3 2.9 copy.26
  90.2 33.9 %while.36 = (s32[]{:T(128)}, f32[4,128,256]{2,1,0:T(8,128)S(1)}, f32[8,4,128,128]{2,3,1,0:T(8,128)}, f32[8,4,128,128]{3,2,1,0:T(8,128)}, f32[8,4,128,128]{3,2,1,0:T(8,128)}, /*index=5*/s32[]{:T(128)}) while((s32[]{:T(128)}, f32[4,128,256]{2,1,0:T(8,128)S(1)}, f32[8,4,128,128]{2,3,1,0:T(8,128)}, f32[8,4,128,128]{3,2,1,0:T(8,128)}, ...), condition=%wide.region_2.3_spmd, body=%wide.region_1.0_spmd.sunk | while | flops 403046400 | bytes 4457545 | solution.py:99
  127.2 5.1 %all-to-all-start.3 = ((bf16[128,32,128]{2,0,1:T(8,128)(2,1)}), bf16[128,32,128]{2,0,1:T(8,128)(2,1)S(1)}, u32[]{:S(2)}, u32[]{:S(2)}) async-start(bf16[128,32,128]{2,0,1:T(8,128)(2,1)} %copy.27), calls=%async_computation.3 | async-start | bytes 2097152 | tf_op jit(solution)/shard_map/all_to_all | solution.py:68
  132.3 15.0 %all-to-all-done.3 = bf16[128,32,128]{2,0,1:T(8,128)(2,1)S(1)} async-done(((bf16[128,32,128]{2,0,1:T(8,128)(2,1)}), bf16[128,32,128]{2,0,1:T(8,128)(2,1)S(1)}, u32[]{:S(2)}, u32[]{:S(2)}) %all-to-all-start.3) | async-done | bytes 1048608 | tf_op jit(solution)/shard_map/all_to_all | solution.py:68
  148.0 2.0 fusion.40
  149.9 6.2 %convolution_select_fusion = f32[8,4,128,128]{3,2,1,0:T(8,128)} fusion(bf16[128,8,4,128]{3,0,2,1:T(8,128)(2,1)S(1)} %bitcast.136, f32[8,4,128]{2,1,0:T(4,128)S(1)} %add_rsqrt_fusion.1, pred[128,128]{1,0:T(8,128)(4,1)S(1)} %iota_compare_fusion, bf16[128,8,4,128]{3,0,2,1:T(8,128)(2,1)S(1)} %bitcast.138, f32[8,4,128]{2,1,0:T(4,128)S(1)} %add_rsqrt_fusion), kind=kOutput, calls=%fused_computation.67 | convolution fusion | flops 807927808 | bytes 4243456 | tf_op jit(solution)/shard_map/vmap(vmap())/dot_general | solution.py:54
  156.1 69.1 %all-gather.5.cloned.1.call-done = f32[128,128,128]{2,1,0:T(8,128)} async-done(((f32[4,128,128]{2,1,0:T(8,128)}), f32[128,128,128]{2,1,0:T(8,128)}) %all-gather.5.cloned.1.call-update) | async-done | bytes 8388624 | tf_op jit(solution)/shard_map/all_gather | solution.py:12
  225.2 98.0 %all-gather.7.cloned.1.call-done = f32[128,128,128]{2,1,0:T(8,128)} async-done(((f32[4,128,128]{2,1,0:T(8,128)}), f32[128,128,128]{2,1,0:T(8,128)}) %all-gather.7.cloned.1.call-update) | async-done | bytes 8388624 | tf_op jit(solution)/shard_map/all_gather | solution.py:12
  323.2 47.4 %while.38 = (s32[]{:T(128)}, f32[4,128,128]{2,1,0:T(8,128)S(1)}, s32[]{:T(128)}, f32[32,4,128,128]{3,2,1,0:T(8,128)}, f32[32,4,128,128]{3,2,1,0:T(8,128)}, /*index=5*/s32[]{:T(128)}, s32[]{:T(128)}) while((s32[]{:T(128)}, f32[4,128,128]{2,1,0:T(8,128)S(1)}, s32[]{:T(128)}, f32[32,4,128,128]{3,2,1,0:T(8,128)}, ...), condition=%wide.region_4.5_spmd.clone, body=%wide.region_3.4_spmd.clone.sunk | while | flops 100925440 | bytes 1837663 | solution.py:22
  370.7 44.7 %while.37 = (s32[]{:T(128)}, f32[4,128,128]{2,1,0:T(8,128)S(1)}, bf16[8,4,128,128]{3,2,0,1:T(8,128)(2,1)S(1)}, f32[8,4,128,128]{2,3,1,0:T(8,128)}, f32[8,4,128,1...) while((s32[]{:T(128)}, f32[4,128,128]{2,1,0:T(8,128)S(1)}, ...), condition=%wide.region_7.8_spmd, body=%wide.region_6.7_spmd.sunk | while | flops 402915328 | bytes 3804253 | solution.py:113
  416.2 20.2 %all_to_all.58 = bf16[1024,4,128]{2,1,0:T(4,128)(2,1)S(1)} all-to-all(bf16[1024,4,128]{2,1,0:T(4,128)(2,1)S(1)} %copy.30), channel_id=1, replica_groups=mesh['outer'=32,'inner'=8] {'inner'}, dimensions={0} | all-to-all | bytes 2097152 | tf_op jit(solution)/shard_map/all_to_all | solution.py:115
  (155 shorter events, 136.8 us)
Async XLA Ops:
  6.5 11.1 %all-to-all-start.1 = ((bf16[128,8,4]{0,2,1:T(4,128)(2,1)}), bf16[128,8,4]{0,2,1:T(4,128)(2,1)S(1)}, u32[]{:S(2)}, u32[]{:S(2)}) async-start(bf16[128,8,4]{0,2,1:T(4,128)(2,1)} %bitcast.145), calls=%async_computation.1 | async-start | bytes 16384 | tf_op jit(solution)/shard_map/all_to_all | solution.py:71
  13.0 8.8 %copy-start.3 = (bf16[128,32,128]{2,1,0:T(8,128)(2,1)S(1)}, bf16[128,32,128]{2,1,0:T(8,128)(2,1)}, u32[]{:S(2)}) copy-start(bf16[128,32,128]{2,1,0:T(8,128)(2,1)} %param.12) | copy-start | bytes 3145732
  17.6 19.3 %all-to-all-start = ((bf16[128,32,128]{2,0,1:T(8,128)(2,1)}), bf16[128,32,128]{2,0,1:T(8,128)(2,1)S(1)}, u32[]{:S(2)}, u32[]{:S(2)}) async-start(bf16[128,32,128]{2,0,1:T(8,128)(2,1)} %copy.24), calls=%async_computation | async-start | bytes 2097152 | tf_op jit(solution)/shard_map/all_to_all | solution.py:69
  36.9 40.5 %all-to-all-start.2 = ((bf16[128,32,128]{2,0,1:T(8,128)(2,1)}), bf16[128,32,128]{2,0,1:T(8,128)(2,1)S(1)}, u32[]{:S(2)}, u32[]{:S(2)}) async-start(bf16[128,32,128]{2,0,1:T(8,128)(2,1)} %copy.25), calls=%async_computation.2 | async-start | bytes 2097152 | tf_op jit(solution)/shard_map/all_to_all | solution.py:70
  41.3 184.0 %all-gather.5.cloned.1.call-start = ((), (), s32[]{:S(2)}) async-start(), calls=%async_computation.5 | async-start | bytes 8650752 | tf_op jit(solution)/shard_map/all_gather | solution.py:12
  72.6 1.3 copy-start
  77.4 2.2 copy-start.1
  77.4 3.0 copy-start.2
  124.1 1.6 copy-start.4
  125.0 198.2 %all-gather.7.cloned.1.call-start = ((), (), s32[]{:S(2)}) async-start(), calls=%async_computation.6 | async-start | bytes 8650752 | tf_op jit(solution)/shard_map/all_gather | solution.py:12
  127.2 20.2 %all-to-all-start.3 = ((bf16[128,32,128]{2,0,1:T(8,128)(2,1)}), bf16[128,32,128]{2,0,1:T(8,128)(2,1)S(1)}, u32[]{:S(2)}, u32[]{:S(2)}) async-start(bf16[128,32,128]{2,0,1:T(8,128)(2,1)} %copy.27), calls=%async_computation.3 | async-start | bytes 2097152 | tf_op jit(solution)/shard_map/all_to_all | solution.py:68
Sparse Core Ops, SparseCore 0:
  125.1 100.0 all-gather.4
  227.8 95.4 all-gather.6
where the time goes:
time: 451 us; the launch traced here: 445 us
  waiting for transfers between devices  198 us (44%)
  matrix products  160 us (35%)
  blocking collectives  20.2 us (4%)
  starting transfers between devices  20.1 us (4%)
  local copies, waits for them, and re-layouts  17.2 us (4%)
  between operations  13.9 us (3%)
  other arithmetic  13.7 us (3%)
    all_gather x2, waiting for transfers between devices, prefix(): everything = jax.tree.map(lambda part: lax.all_gather(part, axis), x)  167 us
    dot_general x32, matrix products, combine_pairs(): jnp.einsum('hij,hjk->hik', trans_b, offset_a, precision=HIGH) + offset_b  45.6 us
    all_to_all x1, blocking collectives, shards(): lax.all_to_all(token_major, 'inner', split_axis=0, concat_axis=1, tiled=T...  20.2 us
    dot_general x6, matrix products, unit_lower_inverse(): inverse = inverse + jnp.dot(inverse, power, precision=HIGH)  15.1 us
    all_to_all x1, waiting for transfers between devices, shards(): lax.all_to_all(query, 'inner', split_axis=1, concat_axis=0, tiled=True)  15 us
    all_to_all x1, waiting for transfers between devices, shards(): lax.all_to_all(keys, 'inner', split_axis=1, concat_axis=0, tiled=True)  13.5 us
    dot_general x8, matrix products, pair_step(): jnp.einsum('hcd,hce->hde', kpart, change, precision=HIGH)  13.3 us
    dot_general x8, matrix products, pair_step(): product = jnp.einsum('hcd,hde->hce', wpart, carried, precision=HIGH)  12.3 us
  transfers between devices with their start and end apart: 6, of which 5 were waited for; matrix products, arithmetic and copies ran while one was open for 11% of the time, Pallas kernels for 0%

commit v1 on v0

--- a/solution.py
+++ b/solution.py
@@ -65,7 +65,12 @@
 
 def shards(query, keys, value, beta):
     qhead, khead, vhead, bhead = (
-        lax.all_to_all(query, "inner", split_axis=1, concat_axis=0, tiled=True),
+        jnp.concatenate(
+            lax.all_to_all(
+                jnp.stack(jnp.split(query, lax.axis_size("inner"), axis=1)), "inner", 0, 0
+            ),
+            axis=0,
+        ),
         lax.all_to_all(keys, "inner", split_axis=1, concat_axis=0, tiled=True),
         lax.all_to_all(value, "inner", split_axis=1, concat_axis=0, tiled=True),
         lax.all_to_all(beta, "inner", split_axis=1, concat_axis=0, tiled=True),

time: 451 us -> 451 us (level)
    unnamed x13 -> x19, local copies, waits for them, and re-layouts: 7.54 us -> 10.9 us
  transfers between devices with their start and end apart: 6 -> 6, of which waited for: 5 -> 5; matrix products, arithmetic and copies ran while one was open for 11% -> 12% of each run, Pallas kernels for 0% -> 0%
where the time goes in v1:
time: 451 us; the launch traced here: 445 us
  waiting for transfers between devices  194 us (43%)
  matrix products  160 us (35%)
  local copies, waits for them, and re-layouts  21.6 us (5%)
  blocking collectives  20.2 us (4%)
  starting transfers between devices  20.1 us (4%)
  between operations  13.9 us (3%)
  other arithmetic  13.7 us (3%)
    all_gather x2, waiting for transfers between devices, prefix(): everything = jax.tree.map(lambda part: lax.all_gather(part, axis), x)  163 us
    dot_general x32, matrix products, combine_pairs(): jnp.einsum('hij,hjk->hik', trans_b, offset_a, precision=HIGH) + offset_b  45.6 us
    all_to_all x1, blocking collectives, shards(): lax.all_to_all(token_major, 'inner', split_axis=0, concat_axis=1, tiled=T...  20.2 us
    dot_general x6, matrix products, unit_lower_inverse(): inverse = inverse + jnp.dot(inverse, power, precision=HIGH)  15.1 us
    all_to_all x1, waiting for transfers between devices, shards(): lax.all_to_all(jnp.stack(jnp.split(query, lax.axis_size('inner'), axis=1)...  15 us
    all_to_all x1, waiting for transfers between devices, shards(): lax.all_to_all(keys, 'inner', split_axis=1, concat_axis=0, tiled=True)  13.5 us
    dot_general x8, matrix products, pair_step(): jnp.einsum('hcd,hce->hde', kpart, change, precision=HIGH)  13.3 us
    dot_general x8, matrix products, pair_step(): product = jnp.einsum('hcd,hde->hce', wpart, carried, precision=HIGH)  12.3 us
  transfers between devices with their start and end apart: 6, of which 5 were waited for; matrix products, arithmetic and copies ran while one was open for 12% of the time, Pallas kernels for 0%

profile of v1, /device:TPU:1, one launch (start us, length us, event | category | flops | bytes accessed | tf_op | source)
XLA Modules:
  0.0 445.4 jit_solution(16557918071611647649)
XLA Ops:
  6.5 6.5 %all-to-all-start.1 = ((bf16[128,8,4]{0,2,1:T(4,128)(2,1)}), bf16[128,8,4]{0,2,1:T(4,128)(2,1)S(1)}, u32[]{:S(2)}, u32[]{:S(2)}) async-start(bf16[128,8,4]{0,2,1:T(4,128)(2,1)} %bitcast.169), calls=%async_computation.1 | async-start | bytes 16384 | tf_op jit(solution)/shard_map/all_to_all | solution.py:76
  13.0 2.7 copy.45
  17.6 4.2 all-to-all-start
  23.4 13.5 %all-to-all-done = bf16[128,32,128]{2,0,1:T(8,128)(2,1)S(1)} async-done(((bf16[128,32,128]{2,0,1:T(8,128)(2,1)}), bf16[128,32,128]{2,0,1:T(8,128)(2,1)S(1)}, u32[]{:S(2)}, u32[]{:S(2)}) %all-to-all-start) | async-done | bytes 1048608 | tf_op jit(solution)/shard_map/all_to_all | solution.py:74
  36.9 4.3 all-to-all-start.2
  41.9 6.5 %fusion.55 = f32[8,4,128,128]{3,2,1,0:T(8,128)S(1)} fusion(bf16[128,8,4,128]{3,0,2,1:T(8,128)(2,1)S(1)} %bitcast.161, f32[8,4,128]{2,1,0:T(4,128)S(1)} %add_rsqrt_fusion.1, f32[8,4,128]{2,1,0:T(4,128)S(1)} %convert_bitcast_fusion.2), kind=kOutput, calls=%fused_computation.67 | convolution fusion | flops 807927808 | bytes 3178496 | tf_op jit(solution)/shard_map/vmap(vmap())/dot_general | solution.py:49
  48.4 2.2 fusion.49
  50.6 2.5 subtract_add_fusion
  53.0 2.0 fusion.81
  55.1 2.0 fusion.83
  57.1 2.2 fusion.82
  59.3 2.2 fusion.84
  61.5 2.3 convolution_add_fusion.5
  63.8 2.0 fusion.86
  65.8 2.2 fusion.85
  68.0 2.0 fusion.87
  70.1 2.5 convolution_add_fusion.4
  73.9 3.5 fusion.88
  77.4 2.2 fusion.57
  80.4 4.3 fusion.35
  84.7 2.6 fusion.78
  87.3 2.9 copy.47
  90.2 33.9 %while.36 = (s32[]{:T(128)}, f32[4,128,256]{2,1,0:T(8,128)S(1)}, f32[8,4,128,128]{2,3,1,0:T(8,128)}, f32[8,4,128,128]{3,2,1,0:T(8,128)}, f32[8,4,128,128]{3,2,1,0:T(8,128)}, /*index=5*/s32[]{:T(128)}) while((s32[]{:T(128)}, f32[4,128,256]{2,1,0:T(8,128)S(1)}, f32[8,4,128,128]{2,3,1,0:T(8,128)}, f32[8,4,128,128]{3,2,1,0:T(8,128)}, ...), condition=%wide.region_2.3_spmd, body=%wide.region_1.0_spmd.sunk | while | flops 403046400 | bytes 4457545 | solution.py:104
  131.6 5.1 %all-to-all-start.3 = ((bf16[8,128,4,128]{3,1,2,0:T(8,128)(2,1)}), bf16[8,128,4,128]{3,1,2,0:T(8,128)(2,1)S(1)}, u32[]{:S(2)}, u32[]{:S(2)}) async-start(bf16[8,128,4,128]{3,1,2,0:T(8,128)(2,1)} %fusion.66), calls=%async_computation.3 | async-start | bytes 2097152 | tf_op jit(solution)/shard_map/all_to_all | solution.py:69
  136.7 15.0 %all-to-all-done.3 = bf16[8,128,4,128]{3,1,2,0:T(8,128)(2,1)S(1)} async-done(((bf16[8,128,4,128]{3,1,2,0:T(8,128)(2,1)}), bf16[8,128,4,128]{3,1,2,0:T(8,128)(2,1)S(1)}, u32[]{:S(2)}, u32[]{:S(2)}) %all-to-all-start.3) | async-done | bytes 1048608 | tf_op jit(solution)/shard_map/all_to_all | solution.py:69
  152.4 2.0 bitcast_multiply_fusion
  154.3 6.2 %convolution_select_fusion = f32[8,4,128,128]{3,2,1,0:T(8,128)} fusion(bf16[128,8,4,128]{3,0,2,1:T(8,128)(2,1)S(1)} %bitcast.162, f32[8,4,128]{2,1,0:T(4,128)S(1)} %add_rsqrt_fusion.1, pred[128,128]{1,0:T(8,128)(4,1)S(1)} %iota_compare_fusion, bf16[8,128,4,128]{3,1,2,0:T(8,128)(2,1)S(1)} %all-to-all-done.3, f32[8,4,128]{2,1,0:T(4,128)S(1)} %add_rsqrt_fusion), kind=kOutput, calls=%fused_computation.66 | convolution fusion | flops 807927808 | bytes 4243456 | tf_op jit(solution)/shard_map/vmap(vmap())/dot_general | solution.py:54
  160.6 64.6 %all-gather.5.cloned.1.call-done = f32[128,128,128]{2,1,0:T(8,128)} async-done(((f32[4,128,128]{2,1,0:T(8,128)}), f32[128,128,128]{2,1,0:T(8,128)}) %all-gather.5.cloned.1.call-update) | async-done | bytes 8388624 | tf_op jit(solution)/shard_map/all_gather | solution.py:12
  225.2 98.0 %all-gather.7.cloned.1.call-done = f32[128,128,128]{2,1,0:T(8,128)} async-done(((f32[4,128,128]{2,1,0:T(8,128)}), f32[128,128,128]{2,1,0:T(8,128)}) %all-gather.7.cloned.1.call-update) | async-done | bytes 8388624 | tf_op jit(solution)/shard_map/all_gather | solution.py:12
  323.2 47.4 %while.38 = (s32[]{:T(128)}, f32[4,128,128]{2,1,0:T(8,128)S(1)}, s32[]{:T(128)}, f32[32,4,128,128]{3,2,1,0:T(8,128)}, f32[32,4,128,128]{3,2,1,0:T(8,128)}, /*index=5*/s32[]{:T(128)}, s32[]{:T(128)}) while((s32[]{:T(128)}, f32[4,128,128]{2,1,0:T(8,128)S(1)}, s32[]{:T(128)}, f32[32,4,128,128]{3,2,1,0:T(8,128)}, ...), condition=%wide.region_4.5_spmd.clone, body=%wide.region_3.4_spmd.clone.sunk | while | flops 100925440 | bytes 1837663 | solution.py:22
  370.6 44.7 %while.37 = (s32[]{:T(128)}, f32[4,128,128]{2,1,0:T(8,128)S(1)}, bf16[8,4,128,128]{3,2,0,1:T(8,128)(2,1)S(1)}, f32[8,4,128,128]{2,3,1,0:T(8,128)}, f32[8,4,128,1...) while((s32[]{:T(128)}, f32[4,128,128]{2,1,0:T(8,128)S(1)}, ...), condition=%wide.region_7.8_spmd, body=%wide.region_6.7_spmd.sunk | while | flops 402915328 | bytes 3804253 | solution.py:118
  416.2 20.2 %all_to_all.54 = bf16[1024,4,128]{2,1,0:T(4,128)(2,1)S(1)} all-to-all(bf16[1024,4,128]{2,1,0:T(4,128)(2,1)S(1)} %copy.58), channel_id=1, replica_groups=mesh['outer'=32,'inner'=8] {'inner'}, dimensions={0} | all-to-all | bytes 2097152 | tf_op jit(solution)/shard_map/all_to_all | solution.py:120
  (163 shorter events, 141.2 us)
Async XLA Ops:
  6.5 11.1 %all-to-all-start.1 = ((bf16[128,8,4]{0,2,1:T(4,128)(2,1)}), bf16[128,8,4]{0,2,1:T(4,128)(2,1)S(1)}, u32[]{:S(2)}, u32[]{:S(2)}) async-start(bf16[128,8,4]{0,2,1:T(4,128)(2,1)} %bitcast.169), calls=%async_computation.1 | async-start | bytes 16384 | tf_op jit(solution)/shard_map/all_to_all | solution.py:76
  13.0 8.8 %copy-start.3 = (bf16[128,32,128]{2,1,0:T(8,128)(2,1)S(1)}, bf16[128,32,128]{2,1,0:T(8,128)(2,1)}, u32[]{:S(2)}) copy-start(bf16[128,32,128]{2,1,0:T(8,128)(2,1)} %param.12) | copy-start | bytes 3145732
  17.6 19.3 %all-to-all-start = ((bf16[128,32,128]{2,0,1:T(8,128)(2,1)}), bf16[128,32,128]{2,0,1:T(8,128)(2,1)S(1)}, u32[]{:S(2)}, u32[]{:S(2)}) async-start(bf16[128,32,128]{2,0,1:T(8,128)(2,1)} %copy.45), calls=%async_computation | async-start | bytes 2097152 | tf_op jit(solution)/shard_map/all_to_all | solution.py:74
  36.9 40.5 %all-to-all-start.2 = ((bf16[128,32,128]{2,0,1:T(8,128)(2,1)}), bf16[128,32,128]{2,0,1:T(8,128)(2,1)S(1)}, u32[]{:S(2)}, u32[]{:S(2)}) async-start(bf16[128,32,128]{2,0,1:T(8,128)(2,1)} %copy.46), calls=%async_computation.2 | async-start | bytes 2097152 | tf_op jit(solution)/shard_map/all_to_all | solution.py:75
  41.3 183.9 %all-gather.5.cloned.1.call-start = ((), (), s32[]{:S(2)}) async-start(), calls=%async_computation.5 | async-start | bytes 8650752 | tf_op jit(solution)/shard_map/all_gather | solution.py:12
  72.6 1.3 copy-start
  77.4 2.2 copy-start.1
  77.4 3.0 copy-start.2
  124.1 1.6 copy-start.4
  125.0 198.2 %all-gather.7.cloned.1.call-start = ((), (), s32[]{:S(2)}) async-start(), calls=%async_computation.6 | async-start | bytes 8650752 | tf_op jit(solution)/shard_map/all_gather | solution.py:12
  131.6 20.2 %all-to-all-start.3 = ((bf16[8,128,4,128]{3,1,2,0:T(8,128)(2,1)}), bf16[8,128,4,128]{3,1,2,0:T(8,128)(2,1)S(1)}, u32[]{:S(2)}, u32[]{:S(2)}) async-start(bf16[8,128,4,128]{3,1,2,0:T(8,128)(2,1)} %fusion.66), calls=%async_computation.3 | async-start | bytes 2097152 | tf_op jit(solution)/shard_map/all_to_all | solution.py:69
Sparse Core Ops, SparseCore 0:
  125.1 100.0 all-gather.4
  227.8 95.4 all-gather.6
